TPU v7x, 512 devices: a whole 4x8x8 slice. The times are simulated.
512 devices in a mesh: row: 32 (over y_hi, z), proto: 16 (over x, y_lo, core).
Axes of the slice: x: 4, y: 8 (y_hi: 4, y_lo: 2; y = y_hi * 2 + y_lo), z: 8, core: 2. Of those that a mesh axis runs over, the one named last changes fastest.
Arguments:
- embeddings: bfloat16 [8192, 128], P('row'), may hold values from -6.75 to 6.75
- second_view: bfloat16 [8192, 128], P('row'), may hold values from -6.75 to 6.75
- prototypes: bfloat16 [65536, 128], P('proto'), may hold values from -6.75 to 6.75
- row_scale: float32 [8192], P('row'), may hold values from 1 to 16, as said below
- col_scale: float32 [65536], P('proto'), may hold values from 1 to 16, as said below
Outputs:
- embed_grad: float32 [8192, 128], P(('row', 'proto'))
- proto_grad: float32 [65536, 128], P(('proto', 'row'))
Inputs may be any that keep to these rules, and one draw needn't show every extreme that they name: `row_scale`: positive scalings. `col_scale`: positive scalings.
All inputs are finite; a program needn't handle non-finite values.
Results may differ from a plain program's by a relative error of at most 0.0025.
Values may be sent and summed in bfloat16 or wider, within the bound.
A program may use at most 64 MiB of HBM per device.

v0:
```python
import jax
import jax.numpy as jnp
from jax import lax
from jax.sharding import PartitionSpec as P

ITERS = 4


def contract_rows(left, right):
    return lax.dot_general(
        left, right, (((0,), (0,)), ((), ())), preferred_element_type=jnp.float32
    )


def contract_width(left, right):
    return lax.dot_general(
        left, right, (((1,), (1,)), ((), ())), preferred_element_type=jnp.float32
    )


def per_device(embeddings, second_view, prototypes, row_scale, col_scale):
    feat_width = embeddings.shape[1]
    proto_count = prototypes.shape[0]
    logit_scale = 1.0 / (0.05 * feat_width)
    view_scale = 1.0 / (0.1 * feat_width)
    plan_mass = 64.0 * proto_count * lax.axis_size("proto")

    def make_plan():
        logits = contract_width(embeddings, prototypes) * logit_scale
        return row_scale[:, None] * col_scale[None, :] * jnp.exp(logits) / plan_mass

    def make_cot():
        return -contract_width(second_view, prototypes) * view_scale

    stored_plan = make_plan()
    cotangent = make_cot()
    weighted = stored_plan * cotangent

    def plan_now():
        return make_plan()

    row_mass, row_weight = lax.psum((stored_plan.sum(1), weighted.sum(1)), "proto")
    row_dual = row_weight / row_mass
    col_mass, col_weight = lax.psum((stored_plan.sum(0), weighted.sum(0)), "row")

    def solve_cols(duals_rows):
        product = lax.psum(jnp.dot(duals_rows, plan_now(), precision=lax.Precision.HIGHEST), "row")
        return (col_weight - product) / col_mass

    col_dual = solve_cols(row_dual)
    for sweep in range(ITERS - 1):
        product = lax.psum(jnp.dot(plan_now(), col_dual, precision=lax.Precision.HIGHEST), "proto")
        row_dual = (row_weight - product) / row_mass
        col_dual = solve_cols(row_dual)
    final_plan, final_cot = (make_plan(), make_cot())
    logit_grad = final_plan * (final_cot - row_dual[:, None] - col_dual[None, :])
    scaled_grad = (logit_scale * logit_grad).astype(jnp.bfloat16)
    scaled_plan = (-view_scale * final_plan).astype(jnp.bfloat16)
    embed_grad = lax.psum_scatter(
        jnp.dot(scaled_grad, prototypes, preferred_element_type=jnp.float32),
        "proto",
        scatter_dimension=0,
        tiled=True,
    )
    stacked = jnp.concatenate((scaled_grad, scaled_plan), 0)
    sources = jnp.concatenate((embeddings, second_view), 0)
    proto_grad = lax.psum_scatter(
        contract_rows(stacked, sources), "row", scatter_dimension=0, tiled=True
    )
    return (embed_grad, proto_grad)


def solution(mesh):
    return jax.shard_map(
        per_device,
        mesh=mesh,
        in_specs=(P("row", None), P("row", None), P("proto", None), P("row"), P("proto")),
        out_specs=(P(("row", "proto"), None), P(("proto", "row"), None)),
        check_vma=False,
    )
```

profile of v0, /device:TPU:2, one launch (start us, length us, event | category | flops | bytes accessed | tf_op | source)
XLA Modules:
  0.0 1084.0 jit_solution(11245116675598459363)
XLA Ops:
  7.2 0.0 copy-start
  7.2 0.0 copy-start.2
  7.2 0.0 reduce-scatter.3.cloned.1.call-start
  7.2 1.2 copy-done
  8.4 1.7 fusion.2
  10.1 0.0 copy-done.2
  10.1 0.0 copy-start.1
  10.1 3.3 multiply_reduce_fusion.1
  13.5 0.0 copy-done.1
  13.5 25.7 %all-reduce.1 = (f32[256]{0:T(256)S(1)}, f32[256]{0:T(256)S(1)}) all-reduce(f32[256]{0:T(256)S(1)} %get-tuple-element.2, f32[256]{0:T(256)S(1)} %get-tuple-element.4), channel_id=1, replica_groups=mesh['row'=32,'proto'=16] {'proto'}, use_global_device_ids=true, to_apply=%region_1.0 | all-reduce | flops 512 | bytes 4096 | tf_op jit(solution)/shard_map/psum | solution.py:42
  39.2 4.3 fusion.14
  43.5 161.7 %all-reduce = (f32[4096]{0:T(1024)S(1)}, f32[4096]{0:T(1024)S(1)}, f32[4096]{0:T(1024)S(1)}) all-reduce(f32[4096]{0:T(1024)S(1)} %get-tuple-element.5, f32[4096]{0:T(1024)S(1)} %get-tuple-element.3, f32[4096]{0:T(1024)S(1)} %bitcast.27), channel_id=1, replica_groups=mesh['row'=32,'proto'=16] {'row'}, use_global_device_ids=true, to_apply=%region_8.0 | all-reduce | flops 12288 | bytes 98304 | tf_op jit(solution)/shard_map/psum | solution.py:44
  205.3 5.5 fusion.12
  210.8 27.1 %psum.82 = f32[256]{0:T(256)S(1)} all-reduce(f32[256]{0:T(256)S(1)} %bitcast.36), channel_id=1, replica_groups=mesh['row'=32,'proto'=16] {'proto'}, use_global_device_ids=true, to_apply=%region_9.0 | all-reduce | flops 256 | bytes 2048 | tf_op jit(solution)/shard_map/psum | solution.py:52
  238.0 4.3 fusion.11
  242.3 152.3 %psum.83 = f32[4096]{0:T(1024)S(1)} all-reduce(f32[4096]{0:T(1024)S(1)} %bitcast.28), channel_id=1, replica_groups=mesh['row'=32,'proto'=16] {'row'}, use_global_device_ids=true, to_apply=%region_10.0 | all-reduce | flops 4096 | bytes 32768 | tf_op jit(solution)/shard_map/psum | solution.py:47
  394.6 5.5 fusion.10
  400.1 27.1 %psum.84 = f32[256]{0:T(256)S(1)} all-reduce(f32[256]{0:T(256)S(1)} %bitcast.37), channel_id=1, replica_groups=mesh['row'=32,'proto'=16] {'proto'}, use_global_device_ids=true, to_apply=%region_11.0 | all-reduce | flops 256 | bytes 2048 | tf_op jit(solution)/shard_map/psum | solution.py:52
  427.3 4.3 fusion.9
  431.6 152.1 %psum.85 = f32[4096]{0:T(1024)S(1)} all-reduce(f32[4096]{0:T(1024)S(1)} %bitcast.29), channel_id=1, replica_groups=mesh['row'=32,'proto'=16] {'row'}, use_global_device_ids=true, to_apply=%region_12.0 | all-reduce | flops 4096 | bytes 32768 | tf_op jit(solution)/shard_map/psum | solution.py:47
  583.8 5.5 fusion.8
  589.3 27.1 %psum.86 = f32[256]{0:T(256)S(1)} all-reduce(f32[256]{0:T(256)S(1)} %bitcast.38), channel_id=1, replica_groups=mesh['row'=32,'proto'=16] {'proto'}, use_global_device_ids=true, to_apply=%region_13.0 | all-reduce | flops 256 | bytes 2048 | tf_op jit(solution)/shard_map/psum | solution.py:52
  616.4 4.3 fusion.7
  620.8 152.3 %psum.87 = f32[4096]{0:T(1024)S(1)} all-reduce(f32[4096]{0:T(1024)S(1)} %bitcast.30), channel_id=1, replica_groups=mesh['row'=32,'proto'=16] {'row'}, use_global_device_ids=true, to_apply=%region_14.0 | all-reduce | flops 4096 | bytes 32768 | tf_op jit(solution)/shard_map/psum | solution.py:47
  773.1 0.0 copy-start.3
  773.1 6.1 multiply_convert_fusion
  779.3 1.4 fusion.27
  780.6 0.0 reduce-scatter.3.cloned.1.call-update
  780.6 0.0 reduce-scatter.5.cloned.1.call-start
  780.7 0.0 copy-done.3
  780.7 4.2 fusion.3
  784.9 0.0 reduce-scatter.5.cloned.1.call-update
  784.9 53.0 %reduce-scatter.3.cloned.1.call-done = f32[16,128]{1,0:T(8,128)} async-done(((f32[256,128]{1,0:T(8,128)}), f32[16,128]{1,0:T(8,128)}) %reduce-scatter.3.cloned.1.call-update) | async-done | bytes 8208 | tf_op jit(solution)/shard_map/reduce_scatter | solution.py:59
  837.9 239.3 %reduce-scatter.5.cloned.1.call-done = f32[128,128]{1,0:T(8,128)} async-done(((f32[4096,128]{1,0:T(8,128)}), f32[128,128]{1,0:T(8,128)}) %reduce-scatter.5.cloned.1.call-update) | async-done | bytes 65552 | tf_op jit(solution)/shard_map/reduce_scatter | solution.py:67
  (8 shorter events, 0.1 us)
Async XLA Ops:
  7.2 1.2 copy-start
  7.2 3.0 copy-start.2
  7.2 830.8 %reduce-scatter.3.cloned.1.call-start = ((), (), s32[]{:S(2)}) async-start(), calls=%async_computation.2 | async-start | bytes 139264 | tf_op jit(solution)/shard_map/reduce_scatter | solution.py:59
  10.1 3.3 copy-start.1
  773.1 7.6 copy-start.3
  780.6 296.6 %reduce-scatter.5.cloned.1.call-start = ((), (), s32[]{:S(2)}) async-start(), calls=%async_computation.3 | async-start | bytes 2162688 | tf_op jit(solution)/shard_map/reduce_scatter | solution.py:67
Sparse Core Ops, SparseCore 0:
  780.8 57.1 reduce-scatter.2
  842.9 234.2 reduce-scatter.4
where the time goes:
time: 1080 us
  blocking collectives  726 us (67%)
  waiting for transfers between devices  292 us (27%)
  matrix products  44.6 us (4%)
  between operations  14.1 us (1%)
    psum x3, blocking collectives, solve_cols(): lax.psum(jnp.dot(duals_rows, plan_now(), precision=lax.Precision.HIGHEST)...  457 us
    reduce_scatter x1, waiting for transfers between devices, per_device(): lax.psum_scatter(contract_rows(stacked, sources), 'row', scatter_dimensio...  239 us
    psum x1, blocking collectives, per_device(): lax.psum((stored_plan.sum(0), weighted.sum(0)), 'row')  162 us
    psum x3, blocking collectives, per_device(): lax.psum(jnp.dot(plan_now(), col_dual, precision=lax.Precision.HIGHEST),...  81.4 us
    reduce_scatter x1, waiting for transfers between devices, per_device(): lax.psum_scatter(jnp.dot(scaled_grad, prototypes, preferred_element_type=...  53 us
    psum x1, blocking collectives, per_device(): lax.psum((stored_plan.sum(1), weighted.sum(1)), 'proto')  25.7 us
  transfers between devices with their start and end apart: 2, of which 2 were waited for; matrix products, arithmetic and copies ran while one was open for 0% of the time, Pallas kernels for 0%

commit v1 on v0

--- a/solution.py
+++ b/solution.py
@@ -44,7 +44,10 @@
     col_mass, col_weight = lax.psum((stored_plan.sum(0), weighted.sum(0)), "row")
 
     def solve_cols(duals_rows):
-        product = lax.psum(jnp.dot(duals_rows, plan_now(), precision=lax.Precision.HIGHEST), "row")
+        product = jnp.sum(
+            lax.all_gather(jnp.dot(duals_rows, plan_now(), precision=lax.Precision.HIGHEST), "row"),
+            axis=0,
+        )
         return (col_weight - product) / col_mass
 
     col_dual = solve_cols(row_dual)

time: 1080 us -> 945 us (0.88)
  blocking collectives: 726 us -> 584 us
    psum x3 -> x0, blocking collectives: 457 us -> none  [solve_cols(): lax.psum(jnp.dot(duals_rows, plan_now(), precision=lax.Precision.HIGHEST)...]
    all_gather x0 -> x4, blocking collectives: none -> 325 us  [solve_cols(): lax.all_gather(jnp.dot(duals_rows, plan_now(), precision=lax.Precision.HI...]
where the time goes in v1:
time: 945 us
  blocking collectives  584 us (62%)
  waiting for transfers between devices  294 us (31%)
  matrix products  44.6 us (5%)
  between operations  14.2 us (2%)
    all_gather x4, blocking collectives, solve_cols(): lax.all_gather(jnp.dot(duals_rows, plan_now(), precision=lax.Precision.HI...  325 us
    reduce_scatter x1, waiting for transfers between devices, per_device(): lax.psum_scatter(contract_rows(stacked, sources), 'row', scatter_dimensio...  239 us
    psum x1, blocking collectives, per_device(): lax.psum((stored_plan.sum(0), weighted.sum(0)), 'row')  152 us
    psum x3, blocking collectives, per_device(): lax.psum(jnp.dot(plan_now(), col_dual, precision=lax.Precision.HIGHEST),...  81.3 us
    reduce_scatter x1, waiting for transfers between devices, per_device(): lax.psum_scatter(jnp.dot(scaled_grad, prototypes, preferred_element_type=...  54.4 us
    psum x1, blocking collectives, per_device(): lax.psum((stored_plan.sum(1), weighted.sum(1)), 'proto')  25.7 us
  transfers between devices with their start and end apart: 2, of which 2 were waited for; matrix products, arithmetic and copies ran while one was open for 0% of the time, Pallas kernels for 0%

profile of v1, /device:TPU:2, one launch (start us, length us, event | category | flops | bytes accessed | tf_op | source)
XLA Modules:
  0.0 944.5 jit_solution(14442879556594504887)
XLA Ops:
  7.2 0.0 copy-start
  7.2 0.0 copy-start.2
  7.2 0.0 reduce-scatter.3.cloned.1.call-start
  7.2 1.2 copy-done
  8.4 1.7 fusion.2
  10.1 0.0 copy-done.2
  10.1 0.0 copy-start.1
  10.1 3.3 multiply_reduce_fusion.1
  13.5 0.0 copy-done.1
  13.5 25.7 %all-reduce.1 = (f32[256]{0:T(256)S(1)}, f32[256]{0:T(256)S(1)}) all-reduce(f32[256]{0:T(256)S(1)} %get-tuple-element.4, f32[256]{0:T(256)S(1)} %get-tuple-element.2), channel_id=1, replica_groups=mesh['row'=32,'proto'=16] {'proto'}, use_global_device_ids=true, to_apply=%region_5.0 | all-reduce | flops 512 | bytes 4096 | tf_op jit(solution)/shard_map/psum | solution.py:42
  39.2 4.3 fusion.14
  43.5 88.1 %all-gather = f32[131072]{0:T(1024)S(1)} all-gather(f32[4096]{0:T(1024)S(1)} %bitcast.27), channel_id=2, replica_groups=mesh['row'=32,'proto'=16] {'row'}, dimensions={0}, use_global_device_ids=true | all-gather | bytes 540672 | tf_op jit(solution)/shard_map/all_gather | solution.py:48
  131.7 0.1 reshape.8
  131.8 152.1 %all-reduce = (f32[4096]{0:T(1024)S(1)}, f32[4096]{0:T(1024)S(1)}) all-reduce(f32[4096]{0:T(1024)S(1)} %get-tuple-element.5, f32[4096]{0:T(1024)S(1)} %get-tuple-element.3), channel_id=1, replica_groups=mesh['row'=32,'proto'=16] {'row'}, use_global_device_ids=true, to_apply=%region_8.0 | all-reduce | flops 8192 | bytes 65536 | tf_op jit(solution)/shard_map/psum | solution.py:44
  283.9 5.5 fusion.12
  289.4 27.1 %psum.53 = f32[256]{0:T(256)S(1)} all-reduce(f32[256]{0:T(256)S(1)} %bitcast.36), channel_id=1, replica_groups=mesh['row'=32,'proto'=16] {'proto'}, use_global_device_ids=true, to_apply=%region_9.0 | all-reduce | flops 256 | bytes 2048 | tf_op jit(solution)/shard_map/psum | solution.py:55
  316.5 4.3 fusion.11
  320.8 78.3 %all-gather.1 = f32[131072]{0:T(1024)S(1)} all-gather(f32[4096]{0:T(1024)S(1)} %bitcast.28), channel_id=3, replica_groups=mesh['row'=32,'proto'=16] {'row'}, dimensions={0}, use_global_device_ids=true | all-gather | bytes 540672 | tf_op jit(solution)/shard_map/all_gather | solution.py:48
  399.1 0.1 reshape.9
  399.2 0.1 reduce_sum.77
  399.3 5.5 fusion.10
  404.8 27.1 %psum.54 = f32[256]{0:T(256)S(1)} all-reduce(f32[256]{0:T(256)S(1)} %bitcast.37), channel_id=1, replica_groups=mesh['row'=32,'proto'=16] {'proto'}, use_global_device_ids=true, to_apply=%region_11.0 | all-reduce | flops 256 | bytes 2048 | tf_op jit(solution)/shard_map/psum | solution.py:55
  432.0 4.3 fusion.9
  436.3 80.2 %all-gather.2 = f32[131072]{0:T(1024)S(1)} all-gather(f32[4096]{0:T(1024)S(1)} %bitcast.29), channel_id=4, replica_groups=mesh['row'=32,'proto'=16] {'row'}, dimensions={0}, use_global_device_ids=true | all-gather | bytes 540672 | tf_op jit(solution)/shard_map/all_gather | solution.py:48
  516.5 0.1 reshape.10
  516.6 0.1 reduce_sum.78
  516.7 5.5 fusion.8
  522.2 27.1 %psum.55 = f32[256]{0:T(256)S(1)} all-reduce(f32[256]{0:T(256)S(1)} %bitcast.38), channel_id=1, replica_groups=mesh['row'=32,'proto'=16] {'proto'}, use_global_device_ids=true, to_apply=%region_13.0 | all-reduce | flops 256 | bytes 2048 | tf_op jit(solution)/shard_map/psum | solution.py:55
  549.4 4.3 fusion.7
  553.7 78.4 %all-gather.3 = f32[131072]{0:T(1024)S(1)} all-gather(f32[4096]{0:T(1024)S(1)} %bitcast.30), channel_id=5, replica_groups=mesh['row'=32,'proto'=16] {'row'}, dimensions={0}, use_global_device_ids=true | all-gather | bytes 540672 | tf_op jit(solution)/shard_map/all_gather | solution.py:48
  632.2 0.1 reshape.11
  632.3 0.1 reduce_sum.79
  632.4 0.0 copy-start.3
  632.4 6.1 multiply_convert_fusion
  638.5 1.3 fusion.27
  639.9 0.0 reduce-scatter.3.cloned.1.call-update
  639.9 0.0 reduce-scatter.5.cloned.1.call-start
  639.9 0.0 copy-done.3
  639.9 4.2 fusion.3
  644.2 0.0 reduce-scatter.5.cloned.1.call-update
  644.2 54.4 %reduce-scatter.3.cloned.1.call-done = f32[16,128]{1,0:T(8,128)} async-done(((f32[256,128]{1,0:T(8,128)}), f32[16,128]{1,0:T(8,128)}) %reduce-scatter.3.cloned.1.call-update) | async-done | bytes 8208 | tf_op jit(solution)/shard_map/reduce_scatter | solution.py:62
  698.7 239.0 %reduce-scatter.5.cloned.1.call-done = f32[128,128]{1,0:T(8,128)} async-done(((f32[4096,128]{1,0:T(8,128)}), f32[128,128]{1,0:T(8,128)}) %reduce-scatter.5.cloned.1.call-update) | async-done | bytes 65552 | tf_op jit(solution)/shard_map/reduce_scatter | solution.py:70
  (9 shorter events, 0.1 us)
Async XLA Ops:
  7.2 1.2 copy-start
  7.2 3.0 copy-start.2
  7.2 691.5 %reduce-scatter.3.cloned.1.call-start = ((), (), s32[]{:S(2)}) async-start(), calls=%async_computation.2 | async-start | bytes 139264 | tf_op jit(solution)/shard_map/reduce_scatter | solution.py:62
  10.1 3.3 copy-start.1
  632.4 7.6 copy-start.3
  639.9 297.8 %reduce-scatter.5.cloned.1.call-start = ((), (), s32[]{:S(2)}) async-start(), calls=%async_computation.3 | async-start | bytes 2162688 | tf_op jit(solution)/shard_map/reduce_scatter | solution.py:70
Sparse Core Ops, SparseCore 0:
  640.0 58.6 reduce-scatter.2
  703.6 233.9 reduce-scatter.4
